TPU v7x, 32 devices: a whole 2x2x4 slice. The times are simulated.
32 devices in a mesh: slab: 4 (over x, core), trace: 8 (over z, y).
Axes of the slice: x: 2, y: 2, z: 4, core: 2. Of those that a mesh axis runs over, the one named last changes fastest.
Arguments:
- incident: float32 [4, 3072, 128], P(None, 'trace'), may hold values from -6 to 6
- green_interior: bfloat16 [4, 2, 4608, 3072], P('slab', None, 'trace'), may hold values from -0.078125 to 0.078125
- green_next: bfloat16 [4, 2, 3072, 3072], P('slab', None, 'trace'), may hold values from -0.0625 to 0.0625
- sources: float32 [4, 4, 3072, 128], P('slab', None, 'trace'), may hold values from -3 to 3
Outputs:
- interior: float32 [4, 4, 4608, 128], P('slab', None, 'trace')
- traces: float32 [4, 4, 3072, 128], P('slab', None, 'trace')
All inputs are finite; a program needn't handle non-finite values.
Results may differ from a plain program's by a relative error of at most 0.014.
Values may be sent and summed in bfloat16 or wider, within the bound.
A program may use at most 64 MiB of HBM per device.

v0:
```python
import functools

import jax
import jax.numpy as jnp
from jax import lax
from jax.experimental import pallas as pl
from jax.experimental.pallas import tpu as pltpu
from jax.sharding import PartitionSpec as P

MESH = pl.DeviceIdType.MESH
INNER = 2


def chunk_count(blocks, rows):
    count = 4
    while count > 1 and (blocks % (count * INNER) or (blocks // count * rows) % 128):
        count //= 2
    return count


def flip(value, mask):
    result = value
    bit = 1
    while bit <= mask:
        if mask & bit:
            result = result + bit - 2 * bit * lax.rem(result // bit, 2)
        bit *= 2
    return result


def visit_order(count):
    return [0] + list(range(count - 1, 0, -1))


def combine(first, second):
    lane = lax.broadcasted_iota(jnp.int32, first.shape, 1)
    half = first.shape[1] // 2
    turned = pltpu.roll(second, half, 1)
    return first + jnp.where(lane < half, -turned, turned)


def kernel(
    slabs,
    blocks,
    incident,
    green_interior,
    green_next,
    sources,
    interior,
    traces,
    entering,
    leaving,
    first_out,
    next_op,
    inner_op,
    incoming,
    own_sources,
    next_sum,
    inner_sum,
    trace_out,
    inner_out,
    recv_sem,
    direct_sem,
    relay_sem,
    load_sem,
    store_sem,
):
    fronts, _, rows, columns = entering.shape
    inner_rows = inner_op.shape[1]
    depth = next_op.shape[2]
    outer = blocks // INNER
    chunks = chunk_count(blocks, rows)
    per_chunk = blocks // chunks
    width = depth // chunks
    slab = lax.axis_index("slab")
    me = lax.axis_index("trace")
    lane_pos = lax.rem(me, INNER)
    my_outer = me // INNER
    partner = me + 1 - 2 * lane_pos
    first_slab = slab == 0
    last_slab = slab == slabs - 1
    my_chunk = me // per_chunk

    def load_incident(front):
        return pltpu.make_async_copy(
            incident.at[front], incoming.at[front], load_sem.at[3 + front]
        )

    load_next = pltpu.make_async_copy(green_next.at[0], next_op, load_sem.at[0])
    load_sources = pltpu.make_async_copy(sources.at[0], own_sources, load_sem.at[1])
    load_inner = pltpu.make_async_copy(green_interior.at[0], inner_op, load_sem.at[2])

    @pl.when(first_slab | last_slab)
    def _():
        for front in range(fronts):
            load_incident(front).start()

    load_next.start()
    load_sources.start()
    load_inner.start()

    barrier = pltpu.get_barrier_semaphore()

    def greet(target_slab, target):
        pl.semaphore_signal(
            barrier, inc=1, device_id={"slab": target_slab, "trace": target}, device_id_type=MESH
        )

    def row_peer(step):
        return flip(my_outer, step) * INNER + lane_pos

    greet(slab, partner)

    @pl.when(first_slab)
    def _():
        for step in range(1, outer):
            greet(slabs - 1, row_peer(step))

    @pl.when(jnp.logical_not(first_slab))
    def _():
        for step in range(outer):
            greet(slab - 1, row_peer(step))

    peers = jnp.where(last_slab, outer, outer + 1)
    pl.semaphore_wait(barrier, peers)

    def first_copy(front, step):
        return pltpu.make_async_remote_copy(
            src_ref=first_out.at[front],
            dst_ref=entering.at[front, me],
            send_sem=direct_sem.at[front, step],
            recv_sem=recv_sem.at[front, me],
            device_id={"slab": 0, "trace": row_peer(step)},
            device_id_type=MESH,
        )

    def next_copy(front, step):
        return pltpu.make_async_remote_copy(
            src_ref=leaving.at[front],
            dst_ref=entering.at[front, me],
            send_sem=direct_sem.at[front, step],
            recv_sem=recv_sem.at[front, me],
            device_id={"slab": slab + 1, "trace": row_peer(step)},
            device_id_type=MESH,
        )

    def relay_copy(front, block):
        return pltpu.make_async_remote_copy(
            src_ref=entering.at[front, block],
            dst_ref=entering.at[front, block],
            send_sem=relay_sem.at[front, block // INNER],
            recv_sem=recv_sem.at[front, block],
            device_id={"slab": slab, "trace": partner},
            device_id_type=MESH,
        )

    def store_trace(front):
        return pltpu.make_async_copy(
            trace_out.at[front], traces.at[0, front], store_sem.at[0, front]
        )

    def store_inner(front):
        return pltpu.make_async_copy(
            inner_out.at[front], interior.at[0, front], store_sem.at[1, front]
        )

    @pl.when(first_slab)
    def _():
        for front in range(fronts):
            load_incident(front).wait()
            entering[front, me] = incoming[front].astype(jnp.bfloat16)

    @pl.when(last_slab)
    def _():
        for front in range(fronts):
            load_incident(front).wait()
            first_out[front] = incoming[front].astype(jnp.bfloat16)
            for step in visit_order(outer)[1:]:
                first_copy(front, step).start()

    def chunk_at(order):
        return flip(my_chunk, visit_order(chunks)[order])

    def vectors(front, chunk):
        return entering[front, pl.ds(chunk * per_chunk, per_chunk)].reshape(width, columns)

    def add_chunk(op, total, front, chunk, fresh):
        start = pl.multiple_of(chunk * width, width)
        halves = op.shape[1]
        matrix = op[:, :, pl.ds(start, width)].reshape(2 * halves, width)
        product = jnp.dot(
            matrix, vectors(front, chunk), preferred_element_type=jnp.float32
        )
        if fresh:
            total[...] = product
        else:
            total[...] += product

    def inner_chunk(front, order):
        add_chunk(inner_op, inner_sum, front, chunk_at(order), order == 0)
        if order == chunks - 1:
            inner_out[front] = combine(inner_sum[0:inner_rows], inner_sum[inner_rows:])
            store_inner(front).start()

    def one_front(front, carry):
        for order in range(chunks):
            for index in range(per_chunk // INNER):
                block = chunk_at(order) * per_chunk + index * INNER + lane_pos

                @pl.when(jnp.logical_not(first_slab & (block == me)))
                def _():
                    relay_copy(front, block).wait_recv()

                relay_copy(front, block).start()

            @pl.when(front > 0)
            def _():
                inner_chunk(front - 1, order)

        @pl.when(front == 0)
        def _():
            load_next.wait()
            load_sources.wait()
            load_inner.wait()

        for order in range(chunks):
            for index in range(per_chunk // INNER):
                block = chunk_at(order) * per_chunk + index * INNER + 1 - lane_pos
                relay_copy(front, block).wait_recv()
            add_chunk(next_op, next_sum, front, chunk_at(order), order == 0)

        result = combine(next_sum[0:rows], next_sum[rows:]) + own_sources[front]
        trace_out[front] = result
        leaving[front] = result.astype(jnp.bfloat16)

        @pl.when(jnp.logical_not(last_slab))
        def _():
            for step in visit_order(outer):
                next_copy(front, step).start()

        store_trace(front).start()
        return carry

    lax.fori_loop(0, fronts, one_front, 0)
    for order in range(chunks):
        inner_chunk(fronts - 1, order)

    def drain(front, carry):
        @pl.when(last_slab)
        def _():
            for step in range(1, outer):
                first_copy(front, step).wait_send()

        @pl.when(jnp.logical_not(last_slab))
        def _():
            for step in range(outer):
                next_copy(front, step).wait_send()

        for index in range(outer):
            relay_copy(front, index * INNER + lane_pos).wait_send()
        store_trace(front).wait()
        store_inner(front).wait()
        return carry

    lax.fori_loop(0, fronts, drain, 0)


def local(slabs, blocks, incident, green_interior, green_next, sources):
    fronts, rows, columns = incident.shape
    inner_rows = green_interior.shape[2]
    depth = green_next.shape[3]
    outer = blocks // INNER
    in_hbm = pl.BlockSpec(memory_space=pltpu.HBM)
    anywhere = pl.BlockSpec(memory_space=pl.ANY)
    return pl.pallas_call(
        functools.partial(kernel, slabs, blocks),
        out_shape=(
            jax.ShapeDtypeStruct((1, fronts, inner_rows, columns), jnp.float32),
            jax.ShapeDtypeStruct((1, fronts, rows, columns), jnp.float32),
        ),
        in_specs=[in_hbm] * 4,
        out_specs=(anywhere, anywhere),
        scratch_shapes=[
            pltpu.VMEM((fronts, blocks, rows, columns), jnp.bfloat16),
            pltpu.VMEM((fronts, rows, columns), jnp.bfloat16),
            pltpu.VMEM((fronts, rows, columns), jnp.bfloat16),
            pltpu.VMEM((2, rows, depth), jnp.bfloat16),
            pltpu.VMEM((2, inner_rows, depth), jnp.bfloat16),
            pltpu.VMEM((fronts, rows, columns), jnp.float32),
            pltpu.VMEM((fronts, rows, columns), jnp.float32),
            pltpu.VMEM((2 * rows, columns), jnp.float32),
            pltpu.VMEM((2 * inner_rows, columns), jnp.float32),
            pltpu.VMEM((fronts, rows, columns), jnp.float32),
            pltpu.VMEM((fronts, inner_rows, columns), jnp.float32),
            pltpu.SemaphoreType.DMA((fronts, blocks)),
            pltpu.SemaphoreType.DMA((fronts, outer)),
            pltpu.SemaphoreType.DMA((fronts, outer)),
            pltpu.SemaphoreType.DMA((3 + fronts,)),
            pltpu.SemaphoreType.DMA((2, fronts)),
        ],
        compiler_params=pltpu.CompilerParams(
            collective_id=0, has_side_effects=True, vmem_limit_bytes=48 * 1024 * 1024
        ),
    )(incident, green_interior, green_next, sources)


def solution(mesh):
    return jax.shard_map(
        functools.partial(local, mesh.shape["slab"], mesh.shape["trace"]),
        mesh=mesh,
        in_specs=(
            P(None, "trace", None),
            P("slab", None, "trace", None),
            P("slab", None, "trace", None),
            P("slab", None, "trace", None),
        ),
        out_specs=(P("slab", None, "trace", None), P("slab", None, "trace", None)),
        check_vma=False,
    )
```

profile of v0, /device:TPU:3, one launch (start us, length us, event | category | flops | bytes accessed | tf_op | source)
XLA Modules:
  0.0 100.6 jit_solution(18191277308163574216)
XLA Ops:
  0.6 0.0 copy-start
  0.6 1.1 %copy-done = f32[4,384,128]{2,1,0:T(8,128)S(1)} copy-done((f32[4,384,128]{2,1,0:T(8,128)S(1)}, f32[4,384,128]{2,1,0:T(8,128)}, u32[]{:S(2)}) %copy-start) | copy-done | bytes 786456
  1.8 0.0 copy-start.1
  1.8 1.1 %copy-done.1 = f32[1,4,384,128]{3,2,1,0:T(8,128)S(1)} copy-done((f32[1,4,384,128]{3,2,1,0:T(8,128)S(1)}, f32[1,4,384,128]{3,2,1,0:T(8,128)}, u32[]{:S(2)}) %copy-start.1) | copy-done | bytes 786456
  2.9 95.8 %shard_map.59 = (f32[1,4,576,128]{3,2,1,0:T(8,128)S(1)}, f32[1,4,384,128]{3,2,1,0:T(8,128)S(1)}) custom-call(f32[4,384,128]{2,1,0:T(8,128)S(1)} %copy-done, bf16[1,2,576,3072]{3,2,1,0:T(8,128)(2,1)} %green_interior.1, bf16[1,2,384,3072]{3,2,1,0:T(8,128)(2,1)} %green_next.1, f32[1,4,384,128]{3,2,1,0:T(8,128)S(1)} %copy-done.1), custom_call_target="tpu_custom_call" | custom-call | tf_op jit(solution)/shard_map/pallas_call | solution.py:275
  98.7 1.0 %copy.8 = f32[1,4,576,128]{3,2,1,0:T(8,128)} copy(f32[1,4,576,128]{3,2,1,0:T(8,128)S(1)} %get-tuple-element.4) | data formatting | bytes 2359296
  99.7 0.9 copy.9
Async XLA Ops:
  0.6 1.1 %copy-start = (f32[4,384,128]{2,1,0:T(8,128)S(1)}, f32[4,384,128]{2,1,0:T(8,128)}, u32[]{:S(2)}) copy-start(f32[4,384,128]{2,1,0:T(8,128)} %incident.1) | copy-start | bytes 2359300
  1.8 1.1 %copy-start.1 = (f32[1,4,384,128]{3,2,1,0:T(8,128)S(1)}, f32[1,4,384,128]{3,2,1,0:T(8,128)}, u32[]{:S(2)}) copy-start(f32[1,4,384,128]{3,2,1,0:T(8,128)} %sources.1) | copy-start | bytes 2359300
where the time goes:
time: 101 us
  Pallas kernels  95.8 us (95%)
  local copies, waits for them, and re-layouts  4.15 us (4%)
    pallas_call x1, Pallas kernels, local(): pl.pallas_call(functools.partial(kernel, slabs, blocks), out_shape=(jax.S...  95.8 us
    unnamed x6, local copies, waits for them, and re-layouts  4.15 us

commit v1 on v0

v1 whole, which is shorter than its diff:
```python
import functools

import jax
import jax.numpy as jnp
from jax import lax
from jax.experimental import pallas as pl
from jax.experimental.pallas import tpu as pltpu
from jax.sharding import PartitionSpec as P

MESH = pl.DeviceIdType.MESH
INNER = 2
HALVES = 2
EARLY = 2
VMEM_LIMIT = 61 * 1024 * 1024


def chunk_count(blocks, rows):
    count = 4
    while count > 1 and (blocks % (count * INNER) or (blocks // count * rows) % 128):
        count //= 2
    return count


def flip(value, mask):
    result = value
    bit = 1
    while bit <= mask:
        if mask & bit:
            result = result + bit - 2 * bit * lax.rem(result // bit, 2)
        bit *= 2
    return result


def visit_order(count):
    return [0] + list(range(count - 1, 0, -1))


def group_of(fronts):
    return 2 if fronts % 2 == 0 else 1


def lanes(shape):
    return lax.broadcasted_iota(jnp.int32, shape, len(shape) - 1)


def turn(value, lead):
    columns = value.shape[-1]
    return pltpu.roll(value, (columns - lead) % columns, len(value.shape) - 1)


def split(value):
    quarter = value.shape[1] // 4
    lower = lanes(value.shape) < quarter
    near, far = turn(value, quarter), turn(value, 2 * quarter)
    return jnp.where(lower, value, near), jnp.where(lower, near, far)


def merge(first, second):
    quarter = first.shape[1] // 4
    lane = lanes(first.shape)
    low = jnp.where(lane < quarter, first, turn(second, -quarter))
    high = jnp.where(lane < 3 * quarter, turn(first, -quarter), turn(second, -2 * quarter))
    return jnp.where(lane < 2 * quarter, low, high)


def pack(value):
    rows, columns = value.shape
    lower, upper = value[: rows // 2], value[rows // 2 :]
    half = columns // 2
    return jnp.where(lanes(lower.shape) < half, lower, turn(upper, half)).astype(jnp.bfloat16)


def swap(packed):
    return pltpu.roll(packed, packed.shape[-1] // 2, len(packed.shape) - 1)


def rotate(first, second):
    quarter = first.shape[1] // 4
    real = lax.rem(lanes(first.shape) // quarter, 2) == 0
    return first + jnp.where(real, -turn(second, quarter), turn(second, -quarter))


def ordered(value):
    quarter = value.shape[1] // 4
    place = lanes(value.shape) // quarter
    return jnp.where(
        place == 1, turn(value, quarter), jnp.where(place == 2, turn(value, -quarter), value)
    )


def kernel(
    slabs,
    blocks,
    incident,
    green_interior,
    green_next,
    sources,
    interior,
    traces,
    entering,
    leaving,
    first_out,
    next_op,
    inner_op,
    incoming,
    own_sources,
    half_sources,
    half_out,
    next_sum,
    inner_sum,
    trace_out,
    inner_out,
    recv_sem,
    first_sem,
    direct_sem,
    relay_sem,
    load_sem,
    store_sem,
):
    parts, _, half_rows, columns = entering.shape
    fronts, rows = incoming.shape[:2]
    group = group_of(fronts)
    inner_rows = inner_op.shape[1]
    depth = next_op.shape[2]
    outer = blocks // INNER
    chunks = chunk_count(blocks, rows)
    per_chunk = blocks // chunks
    width = depth // chunks
    early = min(EARLY, parts)
    slab = lax.axis_index("slab")
    me = lax.axis_index("trace")
    lane_pos = lax.rem(me, INNER)
    my_outer = me // INNER
    partner = me + 1 - 2 * lane_pos
    first_slab = slab == 0
    second_slab = slab == 1
    last_slab = slab == slabs - 1
    my_chunk = me // per_chunk

    def load_incident(front):
        return pltpu.make_async_copy(
            incident.at[front], incoming.at[front], load_sem.at[3 + front]
        )

    load_next = pltpu.make_async_copy(green_next.at[0], next_op, load_sem.at[0])
    load_sources = pltpu.make_async_copy(sources.at[0], own_sources, load_sem.at[1])
    load_inner = pltpu.make_async_copy(green_interior.at[0], inner_op, load_sem.at[2])

    for front in range(fronts):
        load_incident(front).start()
    load_sources.start()
    load_next.start()
    load_inner.start()

    barrier = pltpu.get_barrier_semaphore()

    def greet(target_slab, target):
        pl.semaphore_signal(
            barrier, inc=1, device_id={"slab": target_slab, "trace": target}, device_id_type=MESH
        )

    def row_peer(step):
        return flip(my_outer, step) * INNER + lane_pos

    greet(slab, partner)

    @pl.when(first_slab)
    def _():
        for step in range(1, outer):
            greet(1, row_peer(step))
            greet(slabs - 1, row_peer(step))

    @pl.when(jnp.logical_not(first_slab))
    def _():
        for step in range(outer):
            greet(slab - 1, row_peer(step))

    peers = 1 + jnp.where(last_slab, outer - 1, outer) + jnp.where(second_slab, outer - 1, 0)
    pl.semaphore_wait(barrier, peers)

    def first_copy(part, step):
        return pltpu.make_async_remote_copy(
            src_ref=first_out.at[part],
            dst_ref=entering.at[part, me],
            send_sem=first_sem.at[part, step],
            recv_sem=recv_sem.at[part, me],
            device_id={"slab": 0, "trace": row_peer(step)},
            device_id_type=MESH,
        )

    def next_copy(part, step):
        return pltpu.make_async_remote_copy(
            src_ref=leaving.at[part],
            dst_ref=entering.at[part, me],
            send_sem=direct_sem.at[part, step],
            recv_sem=recv_sem.at[part, me],
            device_id={"slab": slab + 1, "trace": row_peer(step)},
            device_id_type=MESH,
        )

    def relay_copy(part, block):
        return pltpu.make_async_remote_copy(
            src_ref=entering.at[part, block],
            dst_ref=entering.at[part, block],
            send_sem=relay_sem.at[part, block // INNER],
            recv_sem=recv_sem.at[part, block],
            device_id={"slab": slab, "trace": partner},
            device_id_type=MESH,
        )

    def store_trace(front):
        return pltpu.make_async_copy(
            trace_out.at[front], traces.at[0, front], store_sem.at[0, front]
        )

    def store_inner(front):
        return pltpu.make_async_copy(
            inner_out.at[front], interior.at[0, front], store_sem.at[1, front]
        )

    for front in range(fronts):
        load_incident(front).wait()

    @pl.when(first_slab)
    def _():
        for front in range(fronts):
            for index, value in enumerate(split(incoming[front])):
                entering[HALVES * front + index, me] = pack(value)

    def send_first(start, stop):
        for part in range(start, stop):
            first_out[part] = pack(split(incoming[part // HALVES])[part % HALVES])
            for step in visit_order(outer)[1:]:
                first_copy(part, step).start()

    @pl.when(second_slab)
    def _():
        send_first(0, early)

    @pl.when(last_slab)
    def _():
        send_first(early, parts)

    def chunk_at(order):
        return flip(my_chunk, visit_order(chunks)[order])

    def relay_chunk(part, order):
        for index in range(per_chunk // INNER):
            block = chunk_at(order) * per_chunk + index * INNER + lane_pos

            @pl.when(jnp.logical_not(first_slab & (block == me)))
            def _():
                relay_copy(part, block).wait_recv()

            relay_copy(part, block).start()

    def await_relayed(part, order):
        for index in range(per_chunk // INNER):
            block = chunk_at(order) * per_chunk + index * INNER + 1 - lane_pos
            relay_copy(part, block).wait_recv()

    def packed_rows(part, chunk):
        return entering[part, pl.ds(chunk * per_chunk, per_chunk)]

    def stacked(lower, upper):
        return jnp.concatenate([lower, upper], axis=1).reshape(width, columns)

    def matrix_of(op, chunk):
        start = pl.multiple_of(chunk * width, width)
        return op[:, :, pl.ds(start, width)].reshape(2 * op.shape[1], width)

    def next_chunk(part, order):
        chunk = chunk_at(order)
        value = packed_rows(part, chunk)
        product = jnp.dot(
            matrix_of(next_op, chunk),
            stacked(value, swap(value)),
            preferred_element_type=jnp.float32,
        )
        if order == 0:
            next_sum[...] = product
        else:
            next_sum[...] += product

    def inner_chunk(front, chunk, fresh):
        both = []
        for index in range(group):
            low = packed_rows(HALVES * (front + index), chunk)
            high = packed_rows(HALVES * (front + index) + 1, chunk)
            lower = lanes(low.shape) < columns // 2
            both.append(
                stacked(jnp.where(lower, low, swap(high)), jnp.where(lower, swap(low), high))
            )
        product = jnp.dot(
            matrix_of(inner_op, chunk),
            jnp.concatenate(both, axis=1),
            preferred_element_type=jnp.float32,
        )
        if fresh:
            inner_sum[...] = product
        else:
            inner_sum[...] += product

    def inner_finish(front):
        for index in range(group):
            place = pl.ds(index * columns, columns)
            result = rotate(inner_sum[0:inner_rows, place], inner_sum[inner_rows:, place])
            inner_out[front + index] = ordered(result)
            store_inner(front + index).start()

    def inner_group(front):
        inner_chunk(front, 0, True)

        def more(chunk, carry):
            inner_chunk(front, chunk, False)
            return carry

        lax.fori_loop(1, chunks, more, 0)
        inner_finish(front)

    for order in range(chunks):
        relay_chunk(0, order)

    load_sources.wait()
    for front in range(fronts):
        for index, value in enumerate(split(own_sources[front])):
            half_sources[HALVES * front + index] = value
    load_next.wait()
    load_inner.wait()

    def one_part(part, carry):
        closing = part == parts - 1
        side = lax.rem(part, HALVES)
        front = part // HALVES
        for order in range(chunks):
            await_relayed(part, order)
            next_chunk(part, order)

            @pl.when(closing & last_slab)
            def _():
                inner_chunk(fronts - group, chunk_at(order), order == 0)

            @pl.when(jnp.logical_not(closing))
            def _():
                relay_chunk(part + 1, order)

        result = rotate(next_sum[0:rows], next_sum[rows:]) + half_sources[part]
        leaving[part] = pack(result)

        @pl.when(jnp.logical_not(last_slab))
        def _():
            for step in visit_order(outer):
                next_copy(part, step).start()

        half_out[side] = result

        @pl.when(side == HALVES - 1)
        def _():
            trace_out[front] = merge(half_out[0], half_out[1])
            store_trace(front).start()

        full = lax.rem(part, group * HALVES) == group * HALVES - 1

        @pl.when(full & last_slab & jnp.logical_not(closing))
        def _():
            inner_group(front + 1 - group)

        return carry

    lax.fori_loop(0, parts, one_part, 0)

    @pl.when(last_slab)
    def _():
        inner_finish(fronts - group)

    @pl.when(jnp.logical_not(last_slab))
    def _():
        def rest(index, carry):
            inner_group(index * group)
            return carry

        lax.fori_loop(0, fronts // group, rest, 0)

    def drain_first(start, stop):
        for part in range(start, stop):
            for step in range(1, outer):
                first_copy(part, step).wait_send()

    @pl.when(second_slab)
    def _():
        drain_first(0, early)

    @pl.when(last_slab)
    def _():
        drain_first(early, parts)

    def drain(part, carry):
        @pl.when(jnp.logical_not(last_slab))
        def _():
            for step in range(outer):
                next_copy(part, step).wait_send()

        for index in range(outer):
            relay_copy(part, index * INNER + lane_pos).wait_send()
        return carry

    lax.fori_loop(0, parts, drain, 0)
    for front in range(fronts):
        store_trace(front).wait()
        store_inner(front).wait()


def local(slabs, blocks, incident, green_interior, green_next, sources):
    fronts, rows, columns = incident.shape
    parts, half_rows = HALVES * fronts, rows // HALVES
    inner_rows = green_interior.shape[2]
    depth = green_next.shape[3]
    outer = blocks // INNER
    in_hbm = pl.BlockSpec(memory_space=pltpu.HBM)
    anywhere = pl.BlockSpec(memory_space=pl.ANY)
    return pl.pallas_call(
        functools.partial(kernel, slabs, blocks),
        out_shape=(
            jax.ShapeDtypeStruct((1, fronts, inner_rows, columns), jnp.float32),
            jax.ShapeDtypeStruct((1, fronts, rows, columns), jnp.float32),
        ),
        in_specs=[in_hbm] * 4,
        out_specs=(anywhere, anywhere),
        scratch_shapes=[
            pltpu.VMEM((parts, blocks, half_rows, columns), jnp.bfloat16),
            pltpu.VMEM((parts, half_rows, columns), jnp.bfloat16),
            pltpu.VMEM((parts, half_rows, columns), jnp.bfloat16),
            pltpu.VMEM((2, rows, depth), jnp.bfloat16),
            pltpu.VMEM((2, inner_rows, depth), jnp.bfloat16),
            pltpu.VMEM((fronts, rows, columns), jnp.float32),
            pltpu.VMEM((fronts, rows, columns), jnp.float32),
            pltpu.VMEM((parts, rows, columns), jnp.float32),
            pltpu.VMEM((HALVES, rows, columns), jnp.float32),
            pltpu.VMEM((2 * rows, columns), jnp.float32),
            pltpu.VMEM((2 * inner_rows, group_of(fronts) * columns), jnp.float32),
            pltpu.VMEM((fronts, rows, columns), jnp.float32),
            pltpu.VMEM((fronts, inner_rows, columns), jnp.float32),
            pltpu.SemaphoreType.DMA((parts, blocks)),
            pltpu.SemaphoreType.DMA((parts, outer)),
            pltpu.SemaphoreType.DMA((parts, outer)),
            pltpu.SemaphoreType.DMA((parts, outer)),
            pltpu.SemaphoreType.DMA((3 + fronts,)),
            pltpu.SemaphoreType.DMA((2, fronts)),
        ],
        compiler_params=pltpu.CompilerParams(
            collective_id=0, has_side_effects=True, vmem_limit_bytes=VMEM_LIMIT
        ),
    )(incident, green_interior, green_next, sources)


def solution(mesh):
    return jax.shard_map(
        functools.partial(local, mesh.shape["slab"], mesh.shape["trace"]),
        mesh=mesh,
        in_specs=(
            P(None, "trace", None),
            P("slab", None, "trace", None),
            P("slab", None, "trace", None),
            P("slab", None, "trace", None),
        ),
        out_specs=(P("slab", None, "trace", None), P("slab", None, "trace", None)),
        check_vma=False,
    )
```

time: 101 us -> 83.9 us (0.83)
  Pallas kernels: 95.8 us -> 78.6 us
    pallas_call x1, Pallas kernels: 95.8 us -> 78.6 us  [local(): pl.pallas_call(functools.partial(kernel, slabs, blocks), out_shape=(jax.S...]
    unnamed x6 -> x2, local copies, waits for them, and re-layouts: 4.15 us -> 4.42 us
where the time goes in v1:
time: 83.9 us; the launch traced here: 83.7 us
  Pallas kernels  78.6 us (94%)
  local copies, waits for them, and re-layouts  4.42 us (5%)
    pallas_call x1, Pallas kernels, local(): pl.pallas_call(functools.partial(kernel, slabs, blocks), out_shape=(jax.S...  78.6 us
    unnamed x2, local copies, waits for them, and re-layouts  4.42 us

profile of v1, /device:TPU:3, one launch (start us, length us, event | category | flops | bytes accessed | tf_op | source)
XLA Modules:
  0.0 83.7 jit_solution(16402673399733592760)
XLA Ops:
  0.6 78.6 %shard_map.59 = (f32[1,4,576,128]{3,2,1,0:T(8,128)}, f32[1,4,384,128]{3,2,1,0:T(8,128)}) custom-call(f32[4,384,128]{2,1,0:T(8,128)} %incident.1, bf16[1,2,576,3072]{3,2,1,0:T(8,128)(2,1)} %green_interior.1, bf16[1,2,384,3072]{3,2,1,0:T(8,128)(2,1)} %green_next.1, f32[1,4,384,128]{3,2,1,0:T(8,128)} %sources.1), custom_call_target="tpu_custom_call" | custom-call | tf_op jit(solution)/shard_map/pallas_call | solution.py:421
  79.3 2.4 %copy.8 = f32[1,4,576,128]{3,2,1,0:T(8,128)} copy(f32[1,4,576,128]{3,2,1,0:T(8,128)} %get-tuple-element.4) | data formatting | bytes 2359296
  81.6 2.1 %copy.9 = f32[1,4,384,128]{3,2,1,0:T(8,128)} copy(f32[1,4,384,128]{3,2,1,0:T(8,128)} %get-tuple-element.5) | data formatting | bytes 1572864

commit v2 on v1

--- a/solution.py
+++ b/solution.py
@@ -11,7 +11,7 @@
 INNER = 2
 HALVES = 2
 EARLY = 2
-VMEM_LIMIT = 61 * 1024 * 1024
+VMEM_LIMIT = 48 * 1024 * 1024
 
 
 def chunk_count(blocks, rows):
@@ -417,6 +417,8 @@
     depth = green_next.shape[3]
     outer = blocks // INNER
     in_hbm = pl.BlockSpec(memory_space=pltpu.HBM)
+    incident = pltpu.with_memory_space_constraint(incident, pltpu.HBM)
+    sources = pltpu.with_memory_space_constraint(sources, pltpu.HBM)
     anywhere = pl.BlockSpec(memory_space=pl.ANY)
     return pl.pallas_call(
         functools.partial(kernel, slabs, blocks),

time: 83.9 us -> 81.2 us (0.968)
  local copies, waits for them, and re-layouts: 4.42 us -> 1.89 us
    unnamed x2, local copies, waits for them, and re-layouts: 4.42 us -> 1.89 us
where the time goes in v2:
time: 81.2 us; the launch traced here: 81.1 us
  Pallas kernels  78.5 us (97%)
  local copies, waits for them, and re-layouts  1.89 us (2%)
    pallas_call x1, Pallas kernels, local(): pl.pallas_call(functools.partial(kernel, slabs, blocks), out_shape=(jax.S...  78.5 us
    unnamed x2, local copies, waits for them, and re-layouts  1.89 us

profile of v2, /device:TPU:3, one launch (start us, length us, event | category | flops | bytes accessed | tf_op | source)
XLA Modules:
  0.0 81.1 jit_solution(6050610350652803241)
XLA Ops:
  0.6 78.5 %shard_map.59 = (f32[1,4,576,128]{3,2,1,0:T(8,128)S(1)}, f32[1,4,384,128]{3,2,1,0:T(8,128)S(1)}) custom-call(f32[4,384,128]{2,1,0:T(8,128)} %incident.1, bf16[1,2,576,3072]{3,2,1,0:T(8,128)(2,1)} %green_interior.1, bf16[1,2,384,3072]{3,2,1,0:T(8,128)(2,1)} %green_next.1, f32[1,4,384,128]{3,2,1,0:T(8,128)} %sources.1), custom_call_target="tpu_custom_call" | custom-call | tf_op jit(solution)/shard_map/pallas_call | solution.py:423
  79.2 1.0 %copy.8 = f32[1,4,576,128]{3,2,1,0:T(8,128)} copy(f32[1,4,576,128]{3,2,1,0:T(8,128)S(1)} %get-tuple-element.4) | data formatting | bytes 2359296
  80.2 0.9 %copy.9 = f32[1,4,384,128]{3,2,1,0:T(8,128)} copy(f32[1,4,384,128]{3,2,1,0:T(8,128)S(1)} %get-tuple-element.5) | data formatting | bytes 1572864

commit v3 on v2

--- a/solution.py
+++ b/solution.py
@@ -11,6 +11,7 @@
 INNER = 2
 HALVES = 2
 EARLY = 2
+OWN = 4
 VMEM_LIMIT = 48 * 1024 * 1024
 
 
@@ -33,6 +34,10 @@
 
 def visit_order(count):
     return [0] + list(range(count - 1, 0, -1))
+
+
+def compute_order(count):
+    return [0, 1][:count] + list(range(count - 1, 1, -1))
 
 
 def group_of(fronts):
@@ -163,6 +168,7 @@
         return flip(my_outer, step) * INNER + lane_pos
 
     greet(slab, partner)
+    greet(slab, row_peer(1))
 
     @pl.when(first_slab)
     def _():
@@ -172,10 +178,11 @@
 
     @pl.when(jnp.logical_not(first_slab))
     def _():
+        greet(slab - 1, partner)
         for step in range(outer):
             greet(slab - 1, row_peer(step))
 
-    peers = 1 + jnp.where(last_slab, outer - 1, outer) + jnp.where(second_slab, outer - 1, 0)
+    peers = 2 + jnp.where(last_slab, outer - 1, outer + 1) + jnp.where(second_slab, outer - 1, 0)
     pl.semaphore_wait(barrier, peers)
 
     def first_copy(part, step):
@@ -198,6 +205,26 @@
             device_id_type=MESH,
         )
 
+    def side_copy(part):
+        return pltpu.make_async_remote_copy(
+            src_ref=leaving.at[part],
+            dst_ref=entering.at[part, me],
+            send_sem=direct_sem.at[part, outer],
+            recv_sem=recv_sem.at[part, me],
+            device_id={"slab": slab + 1, "trace": partner},
+            device_id_type=MESH,
+        )
+
+    def row_copy(part):
+        return pltpu.make_async_remote_copy(
+            src_ref=entering.at[part, partner],
+            dst_ref=entering.at[part, partner],
+            send_sem=relay_sem.at[part, flip(my_outer, 1)],
+            recv_sem=recv_sem.at[part, partner],
+            device_id={"slab": slab, "trace": row_peer(1)},
+            device_id_type=MESH,
+        )
+
     def relay_copy(part, block):
         return pltpu.make_async_remote_copy(
             src_ref=entering.at[part, block],
@@ -241,23 +268,38 @@
     def _():
         send_first(early, parts)
 
-    def chunk_at(order):
-        return flip(my_chunk, visit_order(chunks)[order])
+    def steps_of(place):
+        span = per_chunk // INNER
+        return range(place * span, (place + 1) * span)
 
     def relay_chunk(part, order):
-        for index in range(per_chunk // INNER):
-            block = chunk_at(order) * per_chunk + index * INNER + lane_pos
-
-            @pl.when(jnp.logical_not(first_slab & (block == me)))
-            def _():
-                relay_copy(part, block).wait_recv()
-
-            relay_copy(part, block).start()
-
-    def await_relayed(part, order):
-        for index in range(per_chunk // INNER):
-            block = chunk_at(order) * per_chunk + index * INNER + 1 - lane_pos
-            relay_copy(part, block).wait_recv()
+        for step in steps_of(visit_order(chunks)[order]):
+            if step == 0:
+
+                @pl.when(first_slab & (part + OWN < parts))
+                def _():
+                    relay_copy(part + OWN, me).start()
+
+                relay_copy(part, partner).wait_recv()
+                row_copy(part).start()
+            elif step > 1:
+                relay_copy(part, row_peer(step)).wait_recv()
+                relay_copy(part, row_peer(step)).start()
+
+    def await_chunk(part, place):
+        for step in steps_of(place):
+            mine = row_peer(step)
+            other = mine + 1 - 2 * lane_pos
+            if step == 0:
+
+                @pl.when(jnp.logical_not(first_slab))
+                def _():
+                    relay_copy(part, mine).wait_recv()
+
+            else:
+                if step == 1:
+                    relay_copy(part, mine).wait_recv()
+                relay_copy(part, other).wait_recv()
 
     def packed_rows(part, chunk):
         return entering[part, pl.ds(chunk * per_chunk, per_chunk)]
@@ -269,15 +311,15 @@
         start = pl.multiple_of(chunk * width, width)
         return op[:, :, pl.ds(start, width)].reshape(2 * op.shape[1], width)
 
-    def next_chunk(part, order):
-        chunk = chunk_at(order)
+    def next_chunk(part, place):
+        chunk = flip(my_chunk, place)
         value = packed_rows(part, chunk)
         product = jnp.dot(
             matrix_of(next_op, chunk),
             stacked(value, swap(value)),
             preferred_element_type=jnp.float32,
         )
-        if order == 0:
+        if place == 0:
             next_sum[...] = product
         else:
             next_sum[...] += product
@@ -318,8 +360,26 @@
         lax.fori_loop(1, chunks, more, 0)
         inner_finish(front)
 
-    for order in range(chunks):
-        relay_chunk(0, order)
+    def relay_ahead(part, order):
+        for lead, mine in leads:
+            step, later = divmod(order + lead, chunks)
+
+            @pl.when(mine & (part + step < parts))
+            def _():
+                relay_chunk(part + step, later)
+
+    @pl.when(first_slab)
+    def _():
+        for part in range(min(OWN, parts)):
+            relay_copy(part, me).start()
+
+    leads = [(6, first_slab), (4, jnp.logical_not(first_slab))]
+    for lead, mine in leads:
+
+        @pl.when(mine)
+        def _():
+            for count in range(lead):
+                relay_chunk(count // chunks, count % chunks)
 
     load_sources.wait()
     for front in range(fronts):
@@ -332,24 +392,24 @@
         closing = part == parts - 1
         side = lax.rem(part, HALVES)
         front = part // HALVES
-        for order in range(chunks):
-            await_relayed(part, order)
-            next_chunk(part, order)
+        for order, place in enumerate(compute_order(chunks)):
+            await_chunk(part, place)
+            next_chunk(part, place)
 
             @pl.when(closing & last_slab)
             def _():
-                inner_chunk(fronts - group, chunk_at(order), order == 0)
-
-            @pl.when(jnp.logical_not(closing))
-            def _():
-                relay_chunk(part + 1, order)
+                inner_chunk(fronts - group, flip(my_chunk, place), order == 0)
+
+            relay_ahead(part, order)
 
         result = rotate(next_sum[0:rows], next_sum[rows:]) + half_sources[part]
         leaving[part] = pack(result)
 
         @pl.when(jnp.logical_not(last_slab))
         def _():
-            for step in visit_order(outer):
+            next_copy(part, 0).start()
+            side_copy(part).start()
+            for step in visit_order(outer)[1:]:
                 next_copy(part, step).start()
 
         half_out[side] = result
@@ -397,11 +457,17 @@
     def drain(part, carry):
         @pl.when(jnp.logical_not(last_slab))
         def _():
+            side_copy(part).wait_send()
             for step in range(outer):
                 next_copy(part, step).wait_send()
 
-        for index in range(outer):
-            relay_copy(part, index * INNER + lane_pos).wait_send()
+        @pl.when(first_slab)
+        def _():
+            relay_copy(part, me).wait_send()
+
+        row_copy(part).wait_send()
+        for step in range(2, outer):
+            relay_copy(part, row_peer(step)).wait_send()
         return carry
 
     lax.fori_loop(0, parts, drain, 0)
@@ -444,7 +510,7 @@
             pltpu.VMEM((fronts, inner_rows, columns), jnp.float32),
             pltpu.SemaphoreType.DMA((parts, blocks)),
             pltpu.SemaphoreType.DMA((parts, outer)),
-            pltpu.SemaphoreType.DMA((parts, outer)),
+            pltpu.SemaphoreType.DMA((parts, outer + 1)),
             pltpu.SemaphoreType.DMA((parts, outer)),
             pltpu.SemaphoreType.DMA((3 + fronts,)),
             pltpu.SemaphoreType.DMA((2, fronts)),

time: 81.2 us -> 79.9 us (0.984)
  Pallas kernels: 78.5 us -> 77.2 us
    pallas_call x1, Pallas kernels: 78.5 us -> 77.2 us  [local(): pl.pallas_call(functools.partial(kernel, slabs, blocks), out_shape=(jax.S...]
where the time goes in v3:
time: 79.9 us; the launch traced here: 79.7 us
  Pallas kernels  77.2 us (97%)
  local copies, waits for them, and re-layouts  1.89 us (2%)
    pallas_call x1, Pallas kernels, local(): pl.pallas_call(functools.partial(kernel, slabs, blocks), out_shape=(jax.S...  77.2 us
    unnamed x2, local copies, waits for them, and re-layouts  1.89 us

profile of v3, /device:TPU:3, one launch (start us, length us, event | category | flops | bytes accessed | tf_op | source)
XLA Modules:
  0.0 79.7 jit_solution(1734758897604432391)
XLA Ops:
  0.6 77.2 %shard_map.59 = (f32[1,4,576,128]{3,2,1,0:T(8,128)S(1)}, f32[1,4,384,128]{3,2,1,0:T(8,128)S(1)}) custom-call(f32[4,384,128]{2,1,0:T(8,128)} %incident.1, bf16[1,2,576,3072]{3,2,1,0:T(8,128)(2,1)} %green_interior.1, bf16[1,2,384,3072]{3,2,1,0:T(8,128)(2,1)} %green_next.1, f32[1,4,384,128]{3,2,1,0:T(8,128)} %sources.1), custom_call_target="tpu_custom_call" | custom-call | tf_op jit(solution)/shard_map/pallas_call | solution.py:489
  77.8 1.0 %copy.8 = f32[1,4,576,128]{3,2,1,0:T(8,128)} copy(f32[1,4,576,128]{3,2,1,0:T(8,128)S(1)} %get-tuple-element.4) | data formatting | bytes 2359296
  78.8 0.9 %copy.9 = f32[1,4,384,128]{3,2,1,0:T(8,128)} copy(f32[1,4,384,128]{3,2,1,0:T(8,128)S(1)} %get-tuple-element.5) | data formatting | bytes 1572864

commit v4 on v3

--- a/solution.py
+++ b/solution.py
@@ -476,6 +476,17 @@
         store_inner(front).wait()
 
 
+def deliver(interior, traces, interior_out, traces_out, sem):
+    copies = []
+    for front in range(traces.shape[1]):
+        copies.append((interior.at[0, front], interior_out.at[0, front], sem.at[0, front]))
+        copies.append((traces.at[0, front], traces_out.at[0, front], sem.at[1, front]))
+    for copy in copies:
+        pltpu.make_async_copy(*copy).start()
+    for copy in copies:
+        pltpu.make_async_copy(*copy).wait()
+
+
 def local(slabs, blocks, incident, green_interior, green_next, sources):
     fronts, rows, columns = incident.shape
     parts, half_rows = HALVES * fronts, rows // HALVES
@@ -486,12 +497,13 @@
     incident = pltpu.with_memory_space_constraint(incident, pltpu.HBM)
     sources = pltpu.with_memory_space_constraint(sources, pltpu.HBM)
     anywhere = pl.BlockSpec(memory_space=pl.ANY)
-    return pl.pallas_call(
+    shapes = (
+        jax.ShapeDtypeStruct((1, fronts, inner_rows, columns), jnp.float32),
+        jax.ShapeDtypeStruct((1, fronts, rows, columns), jnp.float32),
+    )
+    results = pl.pallas_call(
         functools.partial(kernel, slabs, blocks),
-        out_shape=(
-            jax.ShapeDtypeStruct((1, fronts, inner_rows, columns), jnp.float32),
-            jax.ShapeDtypeStruct((1, fronts, rows, columns), jnp.float32),
-        ),
+        out_shape=shapes,
         in_specs=[in_hbm] * 4,
         out_specs=(anywhere, anywhere),
         scratch_shapes=[
@@ -519,6 +531,14 @@
             collective_id=0, has_side_effects=True, vmem_limit_bytes=VMEM_LIMIT
         ),
     )(incident, green_interior, green_next, sources)
+    return pl.pallas_call(
+        deliver,
+        out_shape=shapes,
+        in_specs=[anywhere] * 2,
+        out_specs=(in_hbm, in_hbm),
+        scratch_shapes=[pltpu.SemaphoreType.DMA((2, fronts))],
+        compiler_params=pltpu.CompilerParams(vmem_limit_bytes=1024 * 1024),
+    )(*results)
 
 
 def solution(mesh):

time: 79.9 us -> 79.3 us (level)
  local copies, waits for them, and re-layouts: 1.89 us -> 0 us
  Pallas kernels: 77.2 us -> 78.5 us
    unnamed x2 -> x0, local copies, waits for them, and re-layouts: 1.89 us -> none
    pallas_call x1 -> x2, Pallas kernels: 77.2 us -> 78.5 us  [the longest x1 77.2 us: local(): pl.pallas_call(functools.partial(kernel, slabs, blocks), out_shape=shapes...]
where the time goes in v4:
time: 79.3 us; the launch traced here: 79.2 us
  Pallas kernels  78.5 us (99%)
    pallas_call x1, Pallas kernels, local(): pl.pallas_call(functools.partial(kernel, slabs, blocks), out_shape=shapes...  77.2 us

profile of v4, /device:TPU:3, one launch (start us, length us, event | category | flops | bytes accessed | tf_op | source)
XLA Modules:
  0.0 79.2 jit_solution(2085746453138150858)
XLA Ops:
  0.6 77.2 %shard_map.59 = (f32[1,4,576,128]{3,2,1,0:T(8,128)S(1)}, f32[1,4,384,128]{3,2,1,0:T(8,128)S(1)}) custom-call(f32[4,384,128]{2,1,0:T(8,128)} %incident.1, bf16[1,2,576,3072]{3,2,1,0:T(8,128)(2,1)} %green_interior.1, bf16[1,2,384,3072]{3,2,1,0:T(8,128)(2,1)} %green_next.1, f32[1,4,384,128]{3,2,1,0:T(8,128)} %sources.1), custom_call_target="tpu_custom_call" | custom-call | tf_op jit(solution)/shard_map/pallas_call | solution.py:504
  77.8 1.3 %shard_map.60 = (f32[1,4,576,128]{3,2,1,0:T(8,128)}, f32[1,4,384,128]{3,2,1,0:T(8,128)}) custom-call(f32[1,4,576,128]{3,2,1,0:T(8,128)S(1)} %get-tuple-element.4.interior, f32[1,4,384,128]{3,2,1,0:T(8,128)S(1)} %get-tuple-element.5.traces), custom_call_target="tpu_custom_call" | custom-call | tf_op jit(solution)/shard_map/pallas_call | solution.py:534

commit v5 on v4

--- a/solution.py
+++ b/solution.py
@@ -419,11 +419,27 @@
             trace_out[front] = merge(half_out[0], half_out[1])
             store_trace(front).start()
 
-        full = lax.rem(part, group * HALVES) == group * HALVES - 1
-
-        @pl.when(full & last_slab & jnp.logical_not(closing))
-        def _():
-            inner_group(front + 1 - group)
+        place = lax.rem(part, group * HALVES)
+        prior = (part // (group * HALVES) - 1) * group
+        middle = (chunks + 1) // 2
+        if group > 1:
+
+            @pl.when(last_slab & (prior >= 0) & (place == 0))
+            def _():
+                for chunk in range(middle):
+                    inner_chunk(prior, chunk, chunk == 0)
+
+            @pl.when(last_slab & (prior >= 0) & (place == 1))
+            def _():
+                for chunk in range(middle, chunks):
+                    inner_chunk(prior, chunk, False)
+                inner_finish(prior)
+
+        else:
+
+            @pl.when(last_slab & jnp.logical_not(closing) & (place == HALVES - 1))
+            def _():
+                inner_group(front)
 
         return carry
 

time: 79.3 us -> 79.1 us (level)
  no operation moved by 1% of the time
where the time goes in v5:
time: 79.1 us; the launch traced here: 79 us
  Pallas kernels  78.3 us (99%)
    pallas_call x1, Pallas kernels, local(): pl.pallas_call(functools.partial(kernel, slabs, blocks), out_shape=shapes...  77 us

profile of v5, /device:TPU:3, one launch (start us, length us, event | category | flops | bytes accessed | tf_op | source)
XLA Modules:
  0.0 79.0 jit_solution(10736441186972765738)
XLA Ops:
  0.6 77.0 %shard_map.59 = (f32[1,4,576,128]{3,2,1,0:T(8,128)S(1)}, f32[1,4,384,128]{3,2,1,0:T(8,128)S(1)}) custom-call(f32[4,384,128]{2,1,0:T(8,128)} %incident.1, bf16[1,2,576,3072]{3,2,1,0:T(8,128)(2,1)} %green_interior.1, bf16[1,2,384,3072]{3,2,1,0:T(8,128)(2,1)} %green_next.1, f32[1,4,384,128]{3,2,1,0:T(8,128)} %sources.1), custom_call_target="tpu_custom_call" | custom-call | tf_op jit(solution)/shard_map/pallas_call | solution.py:520
  77.7 1.3 %shard_map.60 = (f32[1,4,576,128]{3,2,1,0:T(8,128)}, f32[1,4,384,128]{3,2,1,0:T(8,128)}) custom-call(f32[1,4,576,128]{3,2,1,0:T(8,128)S(1)} %get-tuple-element.4.interior, f32[1,4,384,128]{3,2,1,0:T(8,128)S(1)} %get-tuple-element.5.traces), custom_call_target="tpu_custom_call" | custom-call | tf_op jit(solution)/shard_map/pallas_call | solution.py:550
